TPU v7x, 32 devices: a whole 2x2x4 slice. The times are simulated.
32 devices in a mesh: slides: 2 (over y), rows: 4 (over z), cols: 2 (over x), chan: 2 (over core).
Axes of the slice: x: 2, y: 2, z: 4, core: 2. Of those that a mesh axis runs over, the one named last changes fastest.
Arguments:
- features: bfloat16 [128, 64, 384], P(('slides', 'rows'), 'cols', 'chan'), parts along dimension 0, may hold values from -6 to 6
- gate_input: bfloat16 [128, 64, 384], P(('slides', 'rows'), 'cols', 'chan'), parts along dimension 0, may hold values from -6 to 6
- decay_idx: int32 [128, 64], P(('slides', 'rows'), 'cols'), parts along dimension 0, may hold values from 0 to 15
- log_table: float32 [16, 384], P(None, 'chan'), may hold values from -1 to 0, as said below
- state_rate: float32 [16], replicated, may hold values from 0.5 to 2
- proj_row: bfloat16 [384, 32], P('chan'), may hold values from -0.0390625 to 0.0390625
- proj_col: bfloat16 [384, 32], P('chan'), may hold values from -0.0390625 to 0.0390625
- conv_w: float32 [3, 3, 384], P(None, None, 'chan'), may hold values from -0.5 to 0.5
- conv_b: float32 [384], P('chan'), may hold values from -0.5 to 0.5
- d_skip: float32 [384], P('chan'), may hold values from 0.5 to 1.5
Outputs:
- output: bfloat16 [128, 64, 384], P(('slides', 'rows'), 'cols', 'chan'), parts along dimension 0
There are 2 independent parts, one for each index of `slides`. A program takes and returns all parts, laid end to end along the dimension named above; an argument that names none is the same for every part. Nothing has to cross between parts.
Inputs may be any that keep to these rules, and one draw needn't show every extreme that they name: `log_table`: every entry is negative.
All inputs are finite; a program needn't handle non-finite values.
Results may differ from a plain program's by a relative error of at most 0.0061.
Values may be sent and summed in bfloat16 or wider, within the bound.
No kernel may reach another device: no remote copies, remote signals or barrier semaphores. Data moves between devices by JAX's collectives and lax.ppermute only.
A program may use at most 128 MiB of HBM per device.

v0:
```python
import jax
import jax.numpy as jnp
from jax import lax
from jax.sharding import PartitionSpec as P


def entering(shard, axis, combine, identity):
    size, position = (lax.axis_size(axis), lax.axis_index(axis))
    everything = jax.tree.map(lambda part: lax.all_gather(part, axis), shard)
    start = jax.tree.map(
        lambda part, zero: jnp.broadcast_to(jnp.asarray(zero, part.dtype), part.shape),
        shard,
        identity,
    )

    def step(k, before):
        reached = k < position
        new = combine(before, jax.tree.map(lambda part: part[k], everything))
        return jax.tree.map(lambda a, b: jnp.where(reached, a, b), new, before)

    return lax.fori_loop(0, size, step, start)


def extended(block, sides, width):
    for axis, dim in sides:
        count = lax.axis_size(axis)
        forward = [(i, i + 1) for i in range(count - 1)]
        backward = [(target, source) for source, target in forward]
        low = lax.ppermute(
            lax.slice_in_dim(block, block.shape[dim] - width, None, axis=dim), axis, forward
        )
        high = lax.ppermute(lax.slice_in_dim(block, 0, width, axis=dim), axis, backward)
        block = jnp.concatenate([low, block, high], axis=dim)
    return block


def combine_pair(earlier, latter):
    return (earlier[0] + latter[0], latter[1] + jnp.exp(latter[0]) * earlier[1])


def make_carry_combine(state_rate):
    rates = state_rate[:, None, None]

    def combine_carry(earlier, latter):
        return (earlier[0] + latter[0], latter[1] + jnp.exp(rates * latter[0][None]) * earlier[1])

    return combine_carry


def lookup(decay_idx, log_table):
    entries = log_table.shape[0]
    onehot = (decay_idx[..., None] == jnp.arange(entries, dtype=jnp.int32)).astype(jnp.float32)
    return jnp.einsum("hwk,ke->hwe", onehot, log_table, precision=lax.Precision.HIGHEST)


def tile_states(values, log_decays, coeffs, state_rate, scan_axis):
    num_states = state_rate.shape[0]
    drive_cols = jnp.moveaxis(coeffs[..., :num_states], -1, 0)[..., None]
    log_sums = jnp.cumsum(log_decays, axis=scan_axis)

    def one_state(inputs):
        state_scale, drive_col = inputs
        unused, states = lax.associative_scan(
            combine_pair, (log_decays * state_scale, drive_col * values), axis=scan_axis
        )
        return states

    return (log_sums, lax.map(one_state, (state_rate, drive_cols)))


def finish(log_sums, states, inflow, coeffs, state_rate):
    num_states = states.shape[0]
    outputs = jnp.moveaxis(coeffs[..., num_states:], -1, 0)[..., None]
    carried = jnp.exp(state_rate[:, None, None, None] * log_sums[None]) * inflow
    return jnp.sum(outputs * (states + carried), axis=0)


def column_coeffs(middle, proj_col):
    return lax.psum(jnp.dot(middle, proj_col, preferred_element_type=jnp.float32), "chan")


def shards(
    features,
    gate_input,
    decay_idx,
    log_table,
    state_rate,
    proj_row,
    proj_col,
    conv_w,
    conv_b,
    d_skip,
):
    combine_carry = make_carry_combine(state_rate)
    log_decays = lookup(decay_idx, log_table)
    feats_wide = features.astype(jnp.float32)
    coeff_row = lax.psum(jnp.dot(features, proj_row, preferred_element_type=jnp.float32), "chan")
    row_sums, states = tile_states(feats_wide, log_decays, coeff_row, state_rate, 1)
    tile_ends = (row_sums[:, -1, :], states[:, :, -1, :])
    incoming = entering(
        tile_ends,
        "cols",
        combine_carry,
        (jnp.zeros_like(tile_ends[0]), jnp.zeros_like(tile_ends[1])),
    )
    swept_rows = finish(row_sums, states, incoming[1][:, :, None, :], coeff_row, state_rate)
    row_out = (swept_rows + d_skip * feats_wide).astype(jnp.bfloat16)
    padded = extended(row_out, (("rows", 0), ("cols", 1)), 1).astype(jnp.float32)
    tile_rows = row_out.shape[0]
    tile_cols = row_out.shape[1]
    convolved = jnp.zeros(row_out.shape, jnp.float32) + conv_b
    for offset_row in range(3):
        for offset_col in range(3):
            convolved = (
                convolved
                + conv_w[offset_row, offset_col]
                * padded[offset_row : offset_row + tile_rows, offset_col : offset_col + tile_cols]
            )
    middle = jax.nn.silu(convolved).astype(jnp.bfloat16)
    strip_vals = lax.all_to_all(middle, "rows", split_axis=1, concat_axis=0, tiled=True)
    strip_index = lax.all_to_all(decay_idx, "rows", split_axis=1, concat_axis=0, tiled=True)
    strip_decays = lookup(strip_index, log_table)
    strip_wide = strip_vals.astype(jnp.float32)
    coeff_col = column_coeffs(strip_vals, proj_col)
    col_sums, states = tile_states(strip_wide, strip_decays, coeff_col, state_rate, 0)
    strip_out = (
        finish(col_sums, states, jnp.zeros((), jnp.float32), coeff_col, state_rate)
        + d_skip * strip_wide
    )
    combined = lax.all_to_all(strip_out, "rows", split_axis=0, concat_axis=1, tiled=True)
    return (combined * jax.nn.silu(gate_input.astype(jnp.float32))).astype(jnp.bfloat16)


def solution(mesh):
    placed = (
        P(("slides", "rows"), "cols", "chan"),
        P(("slides", "rows"), "cols", "chan"),
        P(("slides", "rows"), "cols"),
        P(None, "chan"),
        P(),
        P("chan", None),
        P("chan", None),
        P(None, None, "chan"),
        P("chan"),
        P("chan"),
    )
    return jax.shard_map(
        shards,
        mesh=mesh,
        in_specs=placed,
        out_specs=P(("slides", "rows"), "cols", "chan"),
        check_vma=False,
    )
```

profile of v0, /device:TPU:0, one launch (start us, length us, event | category | flops | bytes accessed | tf_op | source)
XLA Modules:
  0.0 399.4 jit_solution(8053558625621068115)
XLA Ops:
  6.5 1.9 fusion.42
  9.9 6.3 %all-to-all-start.1 = ((s32[4,1,128]{2,1,0:T(1,128)}), s32[4,1,128]{2,1,0:T(1,128)S(1)}, u32[]{:S(2)}, u32[]{:S(2)}) async-start(s32[4,1,128]{2,1,0:T(1,128)} %reshape.23), calls=%async_computation.1 | async-start | bytes 4096 | tf_op jit(solution)/shard_map/all_to_all | solution.py:121
  20.7 4.4 %all-gather.1 = f32[32,1,192]{2,0,1:T(8,128)S(1)} all-gather(f32[16,1,192]{2,0,1:T(8,128)S(1)} %slice.400), channel_id=3, replica_groups=mesh['slides'=2,'rows'=4,'cols'=2,'chan'=2] {'cols'}, dimensions={0}, use_global_device_ids=true | all-gather | bytes 36864 | tf_op jit(solution)/shard_map/all_gather | solution.py:9
  25.1 5.5 %all-reduce.25.cloned.1.call-done = f32[16,32,32]{2,1,0:T(8,128)} async-done(((f32[16,32,32]{2,1,0:T(8,128)}), f32[16,32,32]{2,1,0:T(8,128)}) %all-reduce.25.cloned.1.call-update) | async-done | bytes 65552 | tf_op jit(solution)/shard_map/psum | solution.py:97
  30.6 1.9 slice_bitcast_fusion.3
  33.3 179.7 %while.37 = (s32[]{:T(128)}, f32[16,16,32,192]{3,2,1,0:T(8,128)}, f32[16,16,32,1]{2,1,3,0:T(8,128)}, f32[16,32,192]{2,1,0:T(8,128)}, f32[16]{0:T(128)}, /*index=5*/f32[16,32,192]{2,1,0:T(8,128)S(1)}) while((s32[]{:T(128)}, f32[16,16,32,192]{3,2,1,0:T(8,128)}, f32[16,16,32,1]{2,1,3,0:T(8,128)}, f32[16,32,192]{2,1,0:T(8,128)}, ...), condition=%wide.region_2.3_spmd.clone, body=%wide.region_1.0_spmd.sunk.clone | while | flops 998402 | bytes 15030905 | solution.py:68
  35.3 1.9 broadcast_multiply_fusion.8
  46.5 1.9 broadcast_multiply_fusion.8
  136.3 1.9 broadcast_multiply_fusion.8
  192.4 1.9 broadcast_multiply_fusion.8
  212.9 9.9 %copy.50 = f32[16,16,32,192]{3,1,2,0:T(8,128)S(1)} copy(f32[16,16,32,192]{3,2,1,0:T(8,128)} %get-tuple-element.178) | data formatting | bytes 12582912 | tf_op jit(solution)/shard_map/while | solution.py:68
  223.0 9.5 %all-gather = f32[32,16,1,192]{3,1,2,0:T(8,128)S(1)} all-gather(f32[16,16,1,192]{3,1,2,0:T(8,128)S(1)} %slice.399), channel_id=2, replica_groups=mesh['slides'=2,'rows'=4,'cols'=2,'chan'=2] {'cols'}, dimensions={0}, use_global_device_ids=true | all-gather | bytes 589824 | tf_op jit(solution)/shard_map/all_gather | solution.py:9
  232.9 4.8 %multiply_reduce_fusion.1 = f32[16,32,192]{2,1,0:T(8,128)S(1)} fusion(f32[16,16,32,192]{3,2,1,0:T(8,128)} %get-tuple-element.178, f32[16,16,192]{2,1,0:T(8,128)S(1)} %get-tuple-element.179, f32[16,32,192]{2,1,0:T(8,128)S(1)} %copy-done.4, f32[16]{0:T(128)S(1)} %bitcast.166, f32[16,16,32]{2,1,0:T(8,128)S(1)} %copy.46), kind=kLoop, calls=%fused_computation.70 | loop fusion | flops 7766016 | bytes 7307328 | tf_op jit(solution)/shard_map/reduce_sum | solution.py:75
  237.9 3.7 collective-permute-start
  244.2 3.0 collective-permute-done.1
  247.2 3.4 collective-permute-start.2
  252.0 4.2 %collective-permute-done.3 = bf16[18,1,192]{2,1,0:T(2,128)(2,1)S(1)} collective-permute-done((bf16[18,1,192]{2,1,0:T(2,128)(2,1)S(1)}, bf16[18,1,192]{2,1,0:T(2,128)(2,1)S(1)}, u32[]{:S(2)}, u32[]{:S(2)}) %collective-permute-start.3) | collective-permute-done | bytes 6944 | tf_op jit(solution)/shard_map/ppermute | solution.py:32
  257.8 3.7 all-to-all-start
  262.8 5.4 %all-to-all-done = bf16[16,32,192]{2,0,1:T(8,128)(2,1)S(1)} async-done(((bf16[16,32,192]{2,0,1:T(8,128)(2,1)}), bf16[16,32,192]{2,0,1:T(8,128)(2,1)S(1)}, u32[]{:S(2)}, u32[]{:S(2)}) %all-to-all-start) | async-done | bytes 196640 | tf_op jit(solution)/shard_map/all_to_all | solution.py:120
  269.3 17.2 %all-reduce.27.cloned.1.call-done = f32[64,8,32]{2,1,0:T(8,128)} async-done(((f32[64,8,32]{2,1,0:T(8,128)}), f32[64,8,32]{2,1,0:T(8,128)}) %all-reduce.27.cloned.1.call-update) | async-done | bytes 65552 | tf_op jit(solution)/shard_map/psum | solution.py:79
  286.5 1.9 slice_bitcast_fusion.1
  289.6 76.2 %while.38 = (s32[]{:T(128)}, f32[16,64,8,192]{3,2,1,0:T(8,128)}, f32[16,64,8,1]{2,1,3,0:T(8,128)}, f32[64,8,192]{2,1,0:T(8,128)S(1)}, f32[16]{0:T(128)S(1)}, /*index=5*/f32[64,8,192]{2,1,0:T(8,128)S(1)}) while((s32[]{:T(128)}, f32[16,64,8,192]{3,2,1,0:T(8,128)}, f32[16,64,8,1]{2,1,3,0:T(8,128)}, f32[64,8,192]{2,1,0:T(8,128)S(1)}, ...), condition=%wide.region_9.10_spmd.clone, body=%wide.region_8.9_spmd.sunk.clone | while | flops 1035266 | bytes 11215489 | solution.py:68
  367.3 4.7 %multiply_reduce_fusion = f32[64,8,192]{2,1,0:T(8,128)S(1)} fusion(f32[16,64,8,192]{3,2,1,0:T(8,128)} %get-tuple-element.180, f32[64,8,192]{2,1,0:T(8,128)} %fusion.52, f32[16]{0:T(128)S(1)} %get-tuple-element.646, f32[16,64,8]{2,1,0:T(8,128)S(1)} %copy.53), kind=kLoop, calls=%fused_computation.69 | loop fusion | flops 7766016 | bytes 7110720 | tf_op jit(solution)/shard_map/reduce_sum | solution.py:75
  372.1 19.6 %all_to_all.52 = f32[64,8,192]{2,1,0:T(8,128)S(1)} all-to-all(f32[64,8,192]{2,1,0:T(8,128)S(1)} %multiply_add_fusion.9), channel_id=1, replica_groups=mesh['slides'=2,'rows'=4,'cols'=2,'chan'=2] {'rows'}, dimensions={0} | all-to-all | bytes 786432 | tf_op jit(solution)/shard_map/all_to_all | solution.py:130
  (1557 shorter events, 257.6 us)
Async XLA Ops:
  6.5 9.7 %copy-start = (f32[16,192]{1,0:T(8,128)S(1)}, f32[16,192]{1,0:T(8,128)}, u32[]{:S(2)}) copy-start(f32[16,192]{1,0:T(8,128)} %param.19) | copy-start | bytes 36868
  6.5 24.1 %all-reduce.25.cloned.1.call-start = ((), (), s32[]{:S(2)}) async-start(), calls=%async_computation.3 | async-start | bytes 524288 | tf_op jit(solution)/shard_map/psum | solution.py:97
  9.9 233.0 %all-to-all-start.1 = ((s32[4,1,128]{2,1,0:T(1,128)}), s32[4,1,128]{2,1,0:T(1,128)S(1)}, u32[]{:S(2)}, u32[]{:S(2)}) async-start(s32[4,1,128]{2,1,0:T(1,128)} %reshape.23), calls=%async_computation.1 | async-start | bytes 4096 | tf_op jit(solution)/shard_map/all_to_all | solution.py:121
  212.9 19.5 %copy-start.7 = (f32[16]{0:T(128)S(1)}, f32[16]{0:T(128)}, u32[]{:S(2)}) copy-start(f32[16]{0:T(128)} %get-tuple-element.644) | copy-start | bytes 196
  212.9 19.8 %copy-start.5 = (f32[16,16,32]{0,2,1:T(8,128)S(1)}, f32[16,16,32]{0,2,1:T(8,128)}, u32[]{:S(2)}) copy-start(f32[16,16,32]{0,2,1:T(8,128)} %get-tuple-element.321) | copy-start | bytes 98308
  212.9 20.0 %copy-start.4 = (f32[16,32,192]{2,1,0:T(8,128)S(1)}, f32[16,32,192]{2,1,0:T(8,128)}, u32[]{:S(2)}) copy-start(f32[16,32,192]{2,1,0:T(8,128)} %copy.49) | copy-start | bytes 1179652
  222.9 14.9 %copy-start.3 = (bf16[16,32,192]{2,1,0:T(8,128)(2,1)S(1)}, bf16[16,32,192]{2,1,0:T(8,128)(2,1)}, u32[]{:S(2)}) copy-start(bf16[16,32,192]{2,1,0:T(8,128)(2,1)} %param.16) | copy-start | bytes 589828
  222.9 14.9 %copy-start.10 = (f32[192]{0:T(256)S(1)}, f32[192]{0:T(256)}, u32[]{:S(2)}) copy-start(f32[192]{0:T(256)} %param.25) | copy-start | bytes 2308
  222.9 19.9 %copy-start.9 = (f32[3,3,192]{2,1,0:T(4,128)S(1)}, f32[3,3,192]{2,1,0:T(4,128)}, u32[]{:S(2)}) copy-start(f32[3,3,192]{2,1,0:T(4,128)} %param.23) | copy-start | bytes 20740
  232.4 24.0 %copy-start.11 = (f32[192]{0:T(256)S(1)}, f32[192]{0:T(256)}, u32[]{:S(2)}) copy-start(f32[192]{0:T(256)} %param.24) | copy-start | bytes 2308
  232.9 35.4 %copy-start.8 = (bf16[192,32]{0,1:T(8,128)(2,1)S(1)}, bf16[192,32]{0,1:T(8,128)(2,1)}, u32[]{:S(2)}) copy-start(bf16[192,32]{0,1:T(8,128)(2,1)} %param.22) | copy-start | bytes 36868
  237.9 6.3 %collective-permute-start = (bf16[1,32,192]{2,1,0:T(8,128)(2,1)S(1)}, bf16[1,32,192]{2,1,0:T(8,128)(2,1)S(1)}, u32[]{:S(2)}, u32[]{:S(2)}) collective-permute-start(bf16[1,32,192]{2,1,0:T(8,128)(2,1)S(1)} %get-tuple-element.319), channel_id=1, source_target_pairs={{0,4},{4,8},{8,12},{1,5},{5,9},{9,13},{2,6},{6,10},{10,14},{3,7},{... | collective-permute-start | bytes 36872 | tf_op jit(solution)/shard_map/ppermute | solution.py:29
  241.5 5.6 %collective-permute-start.1 = (bf16[1,32,192]{2,1,0:T(8,128)(2,1)S(1)}, bf16[1,32,192]{2,1,0:T(8,128)(2,1)S(1)}, u32[]{:S(2)}, u32[]{:S(2)}) collective-permute-start(bf16[1,32,192]{2,1,0:T(8,128)(2,1)S(1)} %get-tuple-element.320), channel_id=1, source_target_pairs={{4,0},{8,4},{12,8},{5,1},{9,5},{13,9},{6,2},{10,6},{14,10},{7,3},{... | collective-permute-start | bytes 36872 | tf_op jit(solution)/shard_map/ppermute | solution.py:32
  247.2 4.8 %collective-permute-start.2 = (bf16[18,1,192]{2,1,0:T(2,128)(2,1)S(1)}, bf16[18,1,192]{2,1,0:T(2,128)(2,1)S(1)}, u32[]{:S(2)}, u32[]{:S(2)}) collective-permute-start(bf16[18,1,192]{2,1,0:T(2,128)(2,1)S(1)} %get-tuple-element.315), channel_id=1, source_target_pairs={{0,2},{1,3},{4,6},{5,7},{8,10},{9,11},{12,14},{13,15},{16,18},{17,... | collective-permute-start | bytes 20744 | tf_op jit(solution)/shard_map/ppermute | solution.py:29
  250.6 5.7 %collective-permute-start.3 = (bf16[18,1,192]{2,1,0:T(2,128)(2,1)S(1)}, bf16[18,1,192]{2,1,0:T(2,128)(2,1)S(1)}, u32[]{:S(2)}, u32[]{:S(2)}) collective-permute-start(bf16[18,1,192]{2,1,0:T(2,128)(2,1)S(1)} %get-tuple-element.316), channel_id=1, source_target_pairs={{2,0},{3,1},{6,4},{7,5},{10,8},{11,9},{14,12},{15,13},{18,16},{19,... | collective-permute-start | bytes 20744 | tf_op jit(solution)/shard_map/ppermute | solution.py:32
  257.8 10.5 %all-to-all-start = ((bf16[16,32,192]{2,0,1:T(8,128)(2,1)}), bf16[16,32,192]{2,0,1:T(8,128)(2,1)S(1)}, u32[]{:S(2)}, u32[]{:S(2)}) async-start(bf16[16,32,192]{2,0,1:T(8,128)(2,1)} %copy.51), calls=%async_computation | async-start | bytes 524288 | tf_op jit(solution)/shard_map/all_to_all | solution.py:120
  261.4 25.0 %all-reduce.27.cloned.1.call-start = ((), (), s32[]{:S(2)}) async-start(), calls=%async_computation.4 | async-start | bytes 524288 | tf_op jit(solution)/shard_map/psum | solution.py:79
  268.3 21.3 %copy-start.1 = (bf16[16,4,8,192]{3,2,0,1:T(8,128)(2,1)}, bf16[16,4,8,192]{3,2,0,1:T(8,128)(2,1)S(1)}, u32[]{:S(2)}) copy-start(bf16[16,4,8,192]{3,2,0,1:T(8,128)(2,1)S(1)} %copy.52) | copy-start | bytes 589828
  365.8 6.2 %copy-start.2 = (bf16[16,4,8,192]{3,2,0,1:T(8,128)(2,1)S(1)}, bf16[16,4,8,192]{3,2,0,1:T(8,128)(2,1)}, u32[]{:S(2)}) copy-start(bf16[16,4,8,192]{3,2,0,1:T(8,128)(2,1)} %copy-done.1) | copy-start | bytes 589828
  365.8 25.9 %copy-start.6 = (bf16[16,32,192]{2,1,0:T(8,128)(2,1)S(1)}, bf16[16,32,192]{2,1,0:T(8,128)(2,1)}, u32[]{:S(2)}) copy-start(bf16[16,32,192]{2,1,0:T(8,128)(2,1)} %param.17) | copy-start | bytes 589828
Sparse Core Ops, SparseCore 0:
  9.7 20.9 all-reduce.24
  269.4 17.0 all-reduce.26
where the time goes:
time: 403 us; the launch traced here: 399 us
  local copies, waits for them, and re-layouts  178 us (44%)
  other arithmetic  104 us (26%)
  waiting for transfers between devices  35.4 us (9%)
  blocking collectives  33.5 us (8%)
  starting transfers between devices  19.6 us (5%)
  between operations  13.7 us (3%)
  loops' own time  10.1 us (3%)
  matrix products  4.34 us (1%)
    slice x464, local copies, waits for them, and re-layouts, one_state(): lax.associative_scan(combine_pair, (log_decays * state_scale, drive_col *...  66 us
    mul x32, other arithmetic, one_state(): log_decays * state_scale  41.8 us
    pad x288, local copies, waits for them, and re-layouts, one_state(): lax.associative_scan(combine_pair, (log_decays * state_scale, drive_col *...  36.8 us
    dynamic_slice x32, local copies, waits for them, and re-layouts, tile_states(): return (log_sums, lax.map(one_state, (state_rate, drive_cols)))  30.6 us
    dynamic_update_slice x32, other arithmetic, tile_states(): return (log_sums, lax.map(one_state, (state_rate, drive_cols)))  28.1 us
    mul x32, local copies, waits for them, and re-layouts, one_state(): drive_col * values  23.3 us
    all_to_all x1, blocking collectives, shards(): lax.all_to_all(strip_out, 'rows', split_axis=0, concat_axis=1, tiled=True)  19.6 us
    psum x1, waiting for transfers between devices, column_coeffs(): lax.psum(jnp.dot(middle, proj_col, preferred_element_type=jnp.float32), '...  17.2 us
  transfers between devices with their start and end apart: 8, of which 6 were waited for; matrix products, arithmetic and copies ran while one was open for 50% of the time, Pallas kernels for 0%

commit v1 on v0

--- a/solution.py
+++ b/solution.py
@@ -1,7 +1,23 @@
+import functools
 import jax
 import jax.numpy as jnp
 from jax import lax
 from jax.sharding import PartitionSpec as P
+
+
+def flows_close(state, axis_key):
+    return jnp.concatenate(
+        lax.all_to_all(
+            jnp.stack(jnp.split(state, lax.axis_size(axis_key), axis=0), axis=0),
+            axis_name=axis_key,
+            split_axis=0,
+            concat_axis=0,
+        ),
+        axis=1,
+    )
+
+
+ends_take = functools.partial(flows_close, axis_key="rows")
 
 
 def entering(shard, axis, combine, identity):
@@ -127,7 +143,7 @@
         finish(col_sums, states, jnp.zeros((), jnp.float32), coeff_col, state_rate)
         + d_skip * strip_wide
     )
-    combined = lax.all_to_all(strip_out, "rows", split_axis=0, concat_axis=1, tiled=True)
+    combined = ends_take(strip_out)
     return (combined * jax.nn.silu(gate_input.astype(jnp.float32))).astype(jnp.bfloat16)
 
 

time: 403 us -> 404 us (level)
  no operation moved by 1% of the time
where the time goes in v1:
time: 404 us; the launch traced here: 401 us
  local copies, waits for them, and re-layouts  179 us (44%)
  other arithmetic  105 us (26%)
  waiting for transfers between devices  35.4 us (9%)
  blocking collectives  33.5 us (8%)
  starting transfers between devices  19.6 us (5%)
  between operations  13.7 us (3%)
  loops' own time  10.1 us (2%)
  matrix products  4.34 us (1%)
    slice x464, local copies, waits for them, and re-layouts, one_state(): lax.associative_scan(combine_pair, (log_decays * state_scale, drive_col *...  66 us
    mul x32, other arithmetic, one_state(): log_decays * state_scale  42.3 us
    pad x288, local copies, waits for them, and re-layouts, one_state(): lax.associative_scan(combine_pair, (log_decays * state_scale, drive_col *...  36.8 us
    dynamic_slice x32, local copies, waits for them, and re-layouts, tile_states(): return (log_sums, lax.map(one_state, (state_rate, drive_cols)))  31.2 us
    dynamic_update_slice x32, other arithmetic, tile_states(): return (log_sums, lax.map(one_state, (state_rate, drive_cols)))  28.4 us
    mul x32, local copies, waits for them, and re-layouts, one_state(): drive_col * values  23.3 us
    all_to_all x1, blocking collectives, flows_close(): lax.all_to_all(jnp.stack(jnp.split(state, lax.axis_size(axis_key), axis=0...  19.6 us
    psum x1, waiting for transfers between devices, column_coeffs(): lax.psum(jnp.dot(middle, proj_col, preferred_element_type=jnp.float32), '...  17.2 us
  transfers between devices with their start and end apart: 8, of which 6 were waited for; matrix products, arithmetic and copies ran while one was open for 50% of the time, Pallas kernels for 0%

profile of v1, /device:TPU:0, one launch (start us, length us, event | category | flops | bytes accessed | tf_op | source)
XLA Modules:
  0.0 400.9 jit_solution(7545759124729001668)
XLA Ops:
  6.5 1.9 fusion.42
  9.9 6.3 %all-to-all-start.1 = ((s32[4,1,128]{2,1,0:T(1,128)}), s32[4,1,128]{2,1,0:T(1,128)S(1)}, u32[]{:S(2)}, u32[]{:S(2)}) async-start(s32[4,1,128]{2,1,0:T(1,128)} %reshape.31), calls=%async_computation.1 | async-start | bytes 4096 | tf_op jit(solution)/shard_map/all_to_all | solution.py:137
  20.7 4.4 %all-gather.1 = f32[32,1,192]{2,0,1:T(8,128)S(1)} all-gather(f32[16,1,192]{2,0,1:T(8,128)S(1)} %slice.400), channel_id=3, replica_groups=mesh['slides'=2,'rows'=4,'cols'=2,'chan'=2] {'cols'}, dimensions={0}, use_global_device_ids=true | all-gather | bytes 36864 | tf_op jit(solution)/shard_map/all_gather | solution.py:25
  25.1 5.5 %all-reduce.25.cloned.1.call-done = f32[16,32,32]{2,1,0:T(8,128)} async-done(((f32[16,32,32]{2,1,0:T(8,128)}), f32[16,32,32]{2,1,0:T(8,128)}) %all-reduce.25.cloned.1.call-update) | async-done | bytes 65552 | tf_op jit(solution)/shard_map/psum | solution.py:113
  30.6 1.9 slice_bitcast_fusion.3
  33.3 179.4 %while.37 = (s32[]{:T(128)}, f32[16,16,32,192]{3,2,1,0:T(8,128)}, f32[16,16,32,1]{2,1,3,0:T(8,128)}, f32[16,32,192]{2,1,0:T(8,128)}, f32[16]{0:T(128)}, /*index=5*/f32[16,32,192]{2,1,0:T(8,128)S(1)}) while((s32[]{:T(128)}, f32[16,16,32,192]{3,2,1,0:T(8,128)}, f32[16,16,32,1]{2,1,3,0:T(8,128)}, f32[16,32,192]{2,1,0:T(8,128)}, ...), condition=%wide.region_2.3_spmd.clone, body=%wide.region_1.0_spmd.sunk.clone | while | flops 998402 | bytes 15030905 | solution.py:84
  102.5 1.8 broadcast_multiply_fusion.8
  124.9 1.8 broadcast_multiply_fusion.8
  147.4 1.8 broadcast_multiply_fusion.8
  169.8 1.8 broadcast_multiply_fusion.8
  212.7 9.9 %copy.33 = f32[16,16,32,192]{3,1,2,0:T(8,128)S(1)} copy(f32[16,16,32,192]{3,2,1,0:T(8,128)} %get-tuple-element.178) | data formatting | bytes 12582912 | tf_op jit(solution)/shard_map/while | solution.py:84
  222.7 9.5 %all-gather = f32[32,16,1,192]{3,1,2,0:T(8,128)S(1)} all-gather(f32[16,16,1,192]{3,1,2,0:T(8,128)S(1)} %slice.399), channel_id=2, replica_groups=mesh['slides'=2,'rows'=4,'cols'=2,'chan'=2] {'cols'}, dimensions={0}, use_global_device_ids=true | all-gather | bytes 589824 | tf_op jit(solution)/shard_map/all_gather | solution.py:25
  232.7 4.8 %multiply_reduce_fusion.1 = f32[16,32,192]{2,1,0:T(8,128)S(1)} fusion(f32[16,16,32,192]{3,2,1,0:T(8,128)} %get-tuple-element.178, f32[16,16,192]{2,1,0:T(8,128)S(1)} %get-tuple-element.179, f32[16,32,192]{2,1,0:T(8,128)S(1)} %copy-done.4, f32[16]{0:T(128)S(1)} %bitcast.173, f32[16,16,32]{2,1,0:T(8,128)S(1)} %copy.29), kind=kLoop, calls=%fused_computation.70 | loop fusion | flops 7766016 | bytes 7307328 | tf_op jit(solution)/shard_map/reduce_sum | solution.py:91
  237.6 3.7 collective-permute-start
  243.9 3.0 collective-permute-done.1
  247.0 3.4 collective-permute-start.2
  251.8 4.2 %collective-permute-done.3 = bf16[18,1,192]{2,1,0:T(2,128)(2,1)S(1)} collective-permute-done((bf16[18,1,192]{2,1,0:T(2,128)(2,1)S(1)}, bf16[18,1,192]{2,1,0:T(2,128)(2,1)S(1)}, u32[]{:S(2)}, u32[]{:S(2)}) %collective-permute-start.3) | collective-permute-done | bytes 6944 | tf_op jit(solution)/shard_map/ppermute | solution.py:48
  257.5 3.7 all-to-all-start
  262.6 5.4 %all-to-all-done = bf16[16,32,192]{2,0,1:T(8,128)(2,1)S(1)} async-done(((bf16[16,32,192]{2,0,1:T(8,128)(2,1)}), bf16[16,32,192]{2,0,1:T(8,128)(2,1)S(1)}, u32[]{:S(2)}, u32[]{:S(2)}) %all-to-all-start) | async-done | bytes 196640 | tf_op jit(solution)/shard_map/all_to_all | solution.py:136
  269.1 17.2 %all-reduce.27.cloned.1.call-done = f32[64,8,32]{2,1,0:T(8,128)} async-done(((f32[64,8,32]{2,1,0:T(8,128)}), f32[64,8,32]{2,1,0:T(8,128)}) %all-reduce.27.cloned.1.call-update) | async-done | bytes 65552 | tf_op jit(solution)/shard_map/psum | solution.py:95
  286.2 1.9 slice_bitcast_fusion.1
  289.3 77.8 %while.38 = (s32[]{:T(128)}, f32[16,64,8,192]{3,2,1,0:T(8,128)}, f32[16,64,8,1]{2,1,3,0:T(8,128)}, f32[64,8,192]{2,1,0:T(8,128)S(1)}, f32[16]{0:T(128)S(1)}, /*index=5*/f32[64,8,192]{2,1,0:T(8,128)S(1)}) while((s32[]{:T(128)}, f32[16,64,8,192]{3,2,1,0:T(8,128)}, f32[16,64,8,1]{2,1,3,0:T(8,128)}, f32[64,8,192]{2,1,0:T(8,128)S(1)}, ...), condition=%wide.region_9.10_spmd.clone, body=%wide.region_8.9_spmd.sunk.clone | while | flops 1035266 | bytes 11215489 | solution.py:84
  368.7 4.7 %multiply_reduce_fusion = f32[64,8,192]{2,1,0:T(8,128)S(1)} fusion(f32[16,64,8,192]{3,2,1,0:T(8,128)} %get-tuple-element.180, f32[64,8,192]{2,1,0:T(8,128)} %fusion.52, f32[16]{0:T(128)S(1)} %get-tuple-element.638, f32[16,64,8]{2,1,0:T(8,128)S(1)} %copy.36), kind=kLoop, calls=%fused_computation.69 | loop fusion | flops 7766016 | bytes 7110720 | tf_op jit(solution)/shard_map/reduce_sum | solution.py:91
  373.6 19.6 %all_to_all.39 = f32[4,16,8,192]{3,2,1,0:T(8,128)S(1)} all-to-all(f32[4,16,8,192]{3,2,1,0:T(8,128)S(1)} %pad_maximum_fusion.9), channel_id=1, replica_groups=mesh['slides'=2,'rows'=4,'cols'=2,'chan'=2] {'rows'}, dimensions={0} | all-to-all | bytes 786432 | tf_op jit(solution)/shard_map/all_to_all | solution.py:10
  (1559 shorter events, 259.2 us)
Async XLA Ops:
  6.5 9.7 %copy-start = (f32[16,192]{1,0:T(8,128)S(1)}, f32[16,192]{1,0:T(8,128)}, u32[]{:S(2)}) copy-start(f32[16,192]{1,0:T(8,128)} %param.19) | copy-start | bytes 36868
  6.5 24.1 %all-reduce.25.cloned.1.call-start = ((), (), s32[]{:S(2)}) async-start(), calls=%async_computation.3 | async-start | bytes 524288 | tf_op jit(solution)/shard_map/psum | solution.py:113
  9.9 232.8 %all-to-all-start.1 = ((s32[4,1,128]{2,1,0:T(1,128)}), s32[4,1,128]{2,1,0:T(1,128)S(1)}, u32[]{:S(2)}, u32[]{:S(2)}) async-start(s32[4,1,128]{2,1,0:T(1,128)} %reshape.31), calls=%async_computation.1 | async-start | bytes 4096 | tf_op jit(solution)/shard_map/all_to_all | solution.py:137
  212.7 19.5 %copy-start.7 = (f32[16]{0:T(128)S(1)}, f32[16]{0:T(128)}, u32[]{:S(2)}) copy-start(f32[16]{0:T(128)} %get-tuple-element.636) | copy-start | bytes 196
  212.7 19.8 %copy-start.5 = (f32[16,16,32]{0,2,1:T(8,128)S(1)}, f32[16,16,32]{0,2,1:T(8,128)}, u32[]{:S(2)}) copy-start(f32[16,16,32]{0,2,1:T(8,128)} %get-tuple-element.313) | copy-start | bytes 98308
  212.7 20.0 %copy-start.4 = (f32[16,32,192]{2,1,0:T(8,128)S(1)}, f32[16,32,192]{2,1,0:T(8,128)}, u32[]{:S(2)}) copy-start(f32[16,32,192]{2,1,0:T(8,128)} %copy.32) | copy-start | bytes 1179652
  222.7 14.9 %copy-start.3 = (bf16[16,32,192]{2,1,0:T(8,128)(2,1)S(1)}, bf16[16,32,192]{2,1,0:T(8,128)(2,1)}, u32[]{:S(2)}) copy-start(bf16[16,32,192]{2,1,0:T(8,128)(2,1)} %param.16) | copy-start | bytes 589828
  222.7 14.9 %copy-start.10 = (f32[192]{0:T(256)S(1)}, f32[192]{0:T(256)}, u32[]{:S(2)}) copy-start(f32[192]{0:T(256)} %param.25) | copy-start | bytes 2308
  222.7 19.9 %copy-start.9 = (f32[3,3,192]{2,1,0:T(4,128)S(1)}, f32[3,3,192]{2,1,0:T(4,128)}, u32[]{:S(2)}) copy-start(f32[3,3,192]{2,1,0:T(4,128)} %param.23) | copy-start | bytes 20740
  232.2 24.0 %copy-start.11 = (f32[192]{0:T(256)S(1)}, f32[192]{0:T(256)}, u32[]{:S(2)}) copy-start(f32[192]{0:T(256)} %param.24) | copy-start | bytes 2308
  232.7 35.4 %copy-start.8 = (bf16[192,32]{0,1:T(8,128)(2,1)S(1)}, bf16[192,32]{0,1:T(8,128)(2,1)}, u32[]{:S(2)}) copy-start(bf16[192,32]{0,1:T(8,128)(2,1)} %param.22) | copy-start | bytes 36868
  237.6 6.3 %collective-permute-start = (bf16[1,32,192]{2,1,0:T(8,128)(2,1)S(1)}, bf16[1,32,192]{2,1,0:T(8,128)(2,1)S(1)}, u32[]{:S(2)}, u32[]{:S(2)}) collective-permute-start(bf16[1,32,192]{2,1,0:T(8,128)(2,1)S(1)} %get-tuple-element.311), channel_id=1, source_target_pairs={{0,4},{4,8},{8,12},{1,5},{5,9},{9,13},{2,6},{6,10},{10,14},{3,7},{... | collective-permute-start | bytes 36872 | tf_op jit(solution)/shard_map/ppermute | solution.py:45
  241.3 5.6 %collective-permute-start.1 = (bf16[1,32,192]{2,1,0:T(8,128)(2,1)S(1)}, bf16[1,32,192]{2,1,0:T(8,128)(2,1)S(1)}, u32[]{:S(2)}, u32[]{:S(2)}) collective-permute-start(bf16[1,32,192]{2,1,0:T(8,128)(2,1)S(1)} %get-tuple-element.312), channel_id=1, source_target_pairs={{4,0},{8,4},{12,8},{5,1},{9,5},{13,9},{6,2},{10,6},{14,10},{7,3},{... | collective-permute-start | bytes 36872 | tf_op jit(solution)/shard_map/ppermute | solution.py:48
  247.0 4.8 %collective-permute-start.2 = (bf16[18,1,192]{2,1,0:T(2,128)(2,1)S(1)}, bf16[18,1,192]{2,1,0:T(2,128)(2,1)S(1)}, u32[]{:S(2)}, u32[]{:S(2)}) collective-permute-start(bf16[18,1,192]{2,1,0:T(2,128)(2,1)S(1)} %get-tuple-element.307), channel_id=1, source_target_pairs={{0,2},{1,3},{4,6},{5,7},{8,10},{9,11},{12,14},{13,15},{16,18},{17,... | collective-permute-start | bytes 20744 | tf_op jit(solution)/shard_map/ppermute | solution.py:45
  250.4 5.7 %collective-permute-start.3 = (bf16[18,1,192]{2,1,0:T(2,128)(2,1)S(1)}, bf16[18,1,192]{2,1,0:T(2,128)(2,1)S(1)}, u32[]{:S(2)}, u32[]{:S(2)}) collective-permute-start(bf16[18,1,192]{2,1,0:T(2,128)(2,1)S(1)} %get-tuple-element.308), channel_id=1, source_target_pairs={{2,0},{3,1},{6,4},{7,5},{10,8},{11,9},{14,12},{15,13},{18,16},{19,... | collective-permute-start | bytes 20744 | tf_op jit(solution)/shard_map/ppermute | solution.py:48
  257.5 10.5 %all-to-all-start = ((bf16[16,32,192]{2,0,1:T(8,128)(2,1)}), bf16[16,32,192]{2,0,1:T(8,128)(2,1)S(1)}, u32[]{:S(2)}, u32[]{:S(2)}) async-start(bf16[16,32,192]{2,0,1:T(8,128)(2,1)} %copy.34), calls=%async_computation | async-start | bytes 524288 | tf_op jit(solution)/shard_map/all_to_all | solution.py:136
  261.2 25.0 %all-reduce.27.cloned.1.call-start = ((), (), s32[]{:S(2)}) async-start(), calls=%async_computation.4 | async-start | bytes 524288 | tf_op jit(solution)/shard_map/psum | solution.py:95
  268.1 21.3 %copy-start.1 = (bf16[16,4,8,192]{3,2,0,1:T(8,128)(2,1)}, bf16[16,4,8,192]{3,2,0,1:T(8,128)(2,1)S(1)}, u32[]{:S(2)}) copy-start(bf16[16,4,8,192]{3,2,0,1:T(8,128)(2,1)S(1)} %copy.35) | copy-start | bytes 589828
  367.2 6.2 %copy-start.2 = (bf16[16,4,8,192]{3,2,0,1:T(8,128)(2,1)S(1)}, bf16[16,4,8,192]{3,2,0,1:T(8,128)(2,1)}, u32[]{:S(2)}) copy-start(bf16[16,4,8,192]{3,2,0,1:T(8,128)(2,1)} %copy-done.1) | copy-start | bytes 589828
  367.2 26.0 %copy-start.6 = (bf16[16,32,192]{2,1,0:T(8,128)(2,1)S(1)}, bf16[16,32,192]{2,1,0:T(8,128)(2,1)}, u32[]{:S(2)}) copy-start(bf16[16,32,192]{2,1,0:T(8,128)(2,1)} %param.17) | copy-start | bytes 589828
Sparse Core Ops, SparseCore 0:
  9.7 20.9 all-reduce.24
  269.1 17.0 all-reduce.26
